TPU v7x, 256 devices: a whole 4x4x8 slice. The times are simulated.
256 devices in a mesh: pts: 128 (over x, y, z), rep: 2 (over core).
Axes of the slice: x: 4, y: 4, z: 8, core: 2. Of those that a mesh axis runs over, the one named last changes fastest.
Arguments:
- points: float32 [3, 524288], P(None, ('pts', 'rep')), may hold values from 0 to 1
- scales: float32 [3], replicated, may hold values from 0.1 to 0.3
- pivots: int32 [4, 128], replicated, may hold values from 0 to 524287, as said below
Outputs:
- factor: float32 [512, 524288], P(None, ('pts', 'rep'))
Inputs may be any that keep to these rules, and one draw needn't show every extreme that they name: All 512 indices are distinct. Point i lies on the device whose flat index over pts+rep is i // 2048; no device holds more than 2 pivots of one round, and some device holds exactly 2 in every round.
All inputs are finite; a program needn't handle non-finite values.
Results may differ from a plain program's by a relative error of at most 0.0003.
Values sent between devices are 32-bit elements; how exact they have to be, the bound alone decides.
No kernel may reach another device: no remote copies, remote signals or barrier semaphores. Data moves between devices by JAX's collectives and lax.ppermute only.
A program may use at most 64 MiB of HBM per device.

v0:
```python
import jax
import jax.numpy as jnp
from jax import lax
from jax.sharding import PartitionSpec as P

nugget_level = 0.1


def kernel_block(anchors, targets, inverse):
    squared = jnp.zeros((anchors.shape[1], targets.shape[1]), jnp.float32)
    for component in range(anchors.shape[0]):
        offset = (anchors[component][:, None] - targets[component][None, :]) * inverse[component]
        squared = squared + offset * offset
    return jnp.exp(-0.5 * squared)


def select_rows(sources, index_list, present):
    picked = jnp.concatenate([source[:, index_list] for source in sources], axis=0)
    return picked * present[None, :]


def fetch_rows(sources, chosen, position, point_count):
    pivot_count = chosen.shape[0]
    owner = chosen // point_count
    local_index = chosen - position * point_count
    capacity = 4 * pivot_count // lax.axis_size(("pts", "rep"))
    same_owner = owner[:, None] == owner[None, :]
    earlier = jnp.arange(pivot_count)[None, :] < jnp.arange(pivot_count)[:, None]
    slot_number = jnp.sum((same_owner & earlier).astype(jnp.int32), axis=1)
    owned_here = owner == position
    pick_table = (
        owned_here[:, None] & (slot_number[:, None] == jnp.arange(capacity)[None, :])
    ).astype(jnp.int32)
    slot_local = jnp.sum(pick_table * local_index[:, None], axis=0)
    filled = jnp.sum(pick_table, axis=0).astype(jnp.float32)
    packed = select_rows(sources, slot_local, filled)
    gathered = lax.all_gather(packed, ("pts", "rep"), axis=1, tiled=True)
    return gathered[:, owner * capacity + slot_number]


def per_device(points, scales, pivots):
    point_count = points.shape[1]
    dimension_count = points.shape[0]
    rounds = pivots.shape[0]
    pivot_count = pivots.shape[1]
    position = lax.axis_index(("pts", "rep"))
    inverse = 1.0 / scales
    identity = jnp.eye(pivot_count, dtype=jnp.float32)
    blocks = []
    anchors_seen = []
    factors_seen = []
    history_rows = []
    for round_index in range(rounds):
        chosen = pivots[round_index]
        sources = [points]
        if round_index > 0:
            previous = jnp.concatenate(blocks, axis=0)
            sources = [points, previous]
        fetched = fetch_rows(sources, chosen, position, point_count)
        anchors = fetched[:dimension_count]
        residual = kernel_block(anchors, anchors, inverse) + nugget_level * identity
        columns = kernel_block(anchors, points, inverse)
        if round_index > 0:
            pivot_history = fetched[dimension_count:]
            residual = residual - jnp.dot(
                pivot_history.T, pivot_history, precision=lax.Precision.HIGHEST
            )
            columns = columns - jnp.dot(pivot_history.T, previous, precision=lax.Precision.HIGHEST)
        else:
            pivot_history = jnp.zeros((0, pivot_count), jnp.float32)
        history_rows.append(pivot_history)
        factor = jnp.linalg.cholesky(residual)
        anchors_seen.append(anchors)
        factors_seen.append(factor)
        blocks.append(lax.linalg.triangular_solve(factor, columns, left_side=True, lower=True))
    return jnp.concatenate(blocks, axis=0)


def solution(mesh):
    placed = (P(None, ("pts", "rep")), P(), P())
    return jax.shard_map(
        per_device, mesh=mesh, in_specs=placed, out_specs=P(None, ("pts", "rep")), check_vma=False
    )
```

profile of v0, /device:TPU:1, one launch (start us, length us, event | category | flops | bytes accessed | tf_op | source)
XLA Modules:
  0.0 437.9 jit_solution(6595427470378410402)
XLA Ops:
  6.8 1.1 copy.46
  10.2 67.1 %all-gather = f32[256,2,3]{2,1,0:T(2,128)S(1)} all-gather(f32[1,2,3]{2,1,0:T(2,128)S(1)} %multiply_bitcast_fusion), channel_id=1, replica_groups=mesh['pts'=128,'rep'=2] {'pts','rep'}, dimensions={0}, use_global_device_ids=true | all-gather | bytes 6168 | tf_op jit(solution)/shard_map/all_gather | solution.py:37
  78.2 2.0 select_add_fusion.3
  80.3 2.0 fusion.42
  82.3 11.7 %cholesky.74 = f32[128,128]{1,0:T(8,128)S(1)} custom-call(f32[128,128]{1,0:T(8,128)S(1)} %fusion.42), custom_call_target="Cholesky" | custom-call | tf_op jit(solution)/shard_map/jit(cholesky)/cholesky | solution.py:72
  95.4 9.8 %custom-call.8 = f32[1,128,128]{1,2,0:T(8,128)S(1)} custom-call(f32[1,128,128]{2,1,0:T(8,128)S(1)} %fusion.28), custom_call_target="InvertDiagBlocksLowerTriangular" | custom-call | tf_op jit(solution)/shard_map/triangular_solve/custom-call.0 | solution.py:75
  105.2 3.4 fusion
  109.6 65.9 %all-gather.1 = f32[256,2,131]{2,1,0:T(2,128)S(1)} all-gather(f32[1,2,131]{2,1,0:T(2,128)S(1)} %fusion.51), channel_id=1, replica_groups=mesh['pts'=128,'rep'=2] {'pts','rep'}, dimensions={0}, use_global_device_ids=true | all-gather | bytes 269336 | tf_op jit(solution)/shard_map/all_gather | solution.py:37
  176.8 2.2 convolution_subtract_fusion.4
  179.1 11.7 %cholesky.85 = f32[128,128]{1,0:T(8,128)S(1)} custom-call(f32[128,128]{1,0:T(8,128)S(1)} %fusion.40), custom_call_target="Cholesky" | custom-call | tf_op jit(solution)/shard_map/jit(cholesky)/cholesky | solution.py:72
  192.2 9.8 %custom-call.9 = f32[1,128,128]{1,2,0:T(8,128)S(1)} custom-call(f32[1,128,128]{2,1,0:T(8,128)S(1)} %fusion.29), custom_call_target="InvertDiagBlocksLowerTriangular" | custom-call | tf_op jit(solution)/shard_map/triangular_solve/custom-call.0 | solution.py:75
  202.0 3.3 convolution_subtract_fusion.2
  206.4 1.5 pad_maximum_fusion.2
  207.9 2.9 copy.53
  210.8 2.1 gather_fusion.6
  213.0 78.6 %all-gather.2 = f32[256,2,259]{2,1,0:T(2,128)} all-gather(f32[1,2,259]{2,1,0:T(2,128)S(1)} %fusion.50), channel_id=1, replica_groups=mesh['pts'=128,'rep'=2] {'pts','rep'}, dimensions={0}, use_global_device_ids=true | all-gather | bytes 532504 | tf_op jit(solution)/shard_map/all_gather | solution.py:37
  291.6 1.7 reshape.642
  294.2 2.2 convolution_subtract_fusion.3
  296.6 11.7 %cholesky.96 = f32[128,128]{1,0:T(8,128)S(1)} custom-call(f32[128,128]{1,0:T(8,128)S(1)} %fusion.37), custom_call_target="Cholesky" | custom-call | tf_op jit(solution)/shard_map/jit(cholesky)/cholesky | solution.py:72
  309.6 9.8 %custom-call.10 = f32[1,128,128]{1,2,0:T(8,128)S(1)} custom-call(f32[1,128,128]{2,1,0:T(8,128)S(1)} %fusion.30), custom_call_target="InvertDiagBlocksLowerTriangular" | custom-call | tf_op jit(solution)/shard_map/triangular_solve/custom-call.0 | solution.py:75
  319.5 3.6 convolution_subtract_fusion.1
  324.1 1.9 pad_maximum_fusion.1
  326.0 3.5 copy.57
  329.5 2.4 gather_fusion.9
  332.0 64.7 %all-gather.3 = f32[256,2,387]{2,1,0:T(2,128)} all-gather(f32[1,2,387]{2,1,0:T(2,128)S(1)} %fusion.49), channel_id=1, replica_groups=mesh['pts'=128,'rep'=2] {'pts','rep'}, dimensions={0}, use_global_device_ids=true | all-gather | bytes 795672 | tf_op jit(solution)/shard_map/all_gather | solution.py:37
  396.8 2.9 reshape.644
  399.7 2.1 gather_fusion.10
  402.6 2.3 convolution_subtract_fusion.5
  405.7 12.5 %cholesky.107 = f32[128,128]{1,0:T(8,128)S(1)} custom-call(f32[128,128]{1,0:T(8,128)} %fusion.34), custom_call_target="Cholesky" | custom-call | tf_op jit(solution)/shard_map/jit(cholesky)/cholesky | solution.py:72
  419.6 9.8 %custom-call.11 = f32[1,128,128]{1,2,0:T(8,128)S(1)} custom-call(f32[1,128,128]{2,1,0:T(8,128)S(1)} %fusion.31), custom_call_target="InvertDiagBlocksLowerTriangular" | custom-call | tf_op jit(solution)/shard_map/triangular_solve/custom-call.0 | solution.py:75
  429.4 4.9 %convolution_subtract_fusion = f32[128,2048]{1,0:T(8,128)S(1)} fusion(f32[128]{0:T(128)} %copy-done.2, f32[128]{0:T(128)} %copy-done.3, f32[128]{0:T(128)} %copy-done.1, f32[]{:T(128)} %bitcast.13, f32[2048]{0:T(1024)} %bitcast.235, f32[]{:T(128)} %bitcast.12, f32[2048]{0:T(1024)S(1)} %bitcast.231, f32[]{:T(128)} %bitcast.11, f32[2048]{0:T(1024)S(1)} %bitcast.227, ...), kind=kOutput, calls=%fused_computation.13 | convolution fusion | flops 1212940288 | bytes 4417036 | tf_op jit(solution)/shard_map/dot_general | solution.py:68
  435.4 2.3 pad_maximum_fusion
  (77 shorter events, 23.5 us)
Async XLA Ops:
  6.8 312.7 %copy-start = (f32[1,2048]{1,0:T(1,128)}, f32[1,2048]{1,0:T(1,128)S(1)}, u32[]{:S(2)}) copy-start(f32[1,2048]{1,0:T(1,128)S(1)} %get-tuple-element.37) | copy-start | bytes 24580
  402.0 0.5 copy-start.1
  402.0 0.6 copy-start.2
  402.0 0.6 copy-start.3
where the time goes:
time: 446 us; the launch traced here: 438 us
  blocking collectives  276 us (62%)
  other arithmetic  108 us (24%)
  local copies, waits for them, and re-layouts  27.9 us (6%)
  matrix products  25.2 us (6%)
    all_gather x4, blocking collectives, fetch_rows(): gathered = lax.all_gather(packed, ('pts', 'rep'), axis=1, tiled=True)  276 us
    another operation x12, other arithmetic, per_device(): factor = jnp.linalg.cholesky(residual)  50.4 us
    another operation x8, other arithmetic, per_device(): lax.linalg.triangular_solve(factor, columns, left_side=True, lower=True)  41.9 us
    dot_general x3, matrix products, per_device(): jnp.dot(pivot_history.T, previous, precision=lax.Precision.HIGHEST)  11.9 us

commit v1 on v0

v1 whole, which is shorter than its diff:
```python
import functools
import math

import jax
import jax.numpy as jnp
from jax import lax
from jax.experimental import pallas as pl
from jax.experimental.pallas import tpu as pltpu
from jax.sharding import PartitionSpec as P

nugget_level = 0.1
root_factor = math.sqrt(0.5 * math.log2(math.e))
f32 = jnp.float32
bf16 = jnp.bfloat16
HIGHEST = lax.Precision.HIGHEST


def iota(shape, axis):
    return lax.broadcasted_iota(jnp.int32, shape, axis)


def across_lanes(x, j):
    return jnp.broadcast_to(x[:, j : j + 1], (8, 128))


def across_rows(x, k):
    return jnp.broadcast_to(x[k : k + 1, :], (8, 128))


def pack_kernel(place_ref, points_ref, pivots_ref, out_ref):
    point_count = points_ref.shape[1]
    base = place_ref[0] * point_count
    sub, lane = iota((8, 128), 0), iota((8, 128), 1)
    spread = jnp.zeros((8, 128), jnp.int32)
    for round_index in range(pivots_ref.shape[0]):
        row = jnp.broadcast_to(pivots_ref[round_index : round_index + 1, :], (8, 128))
        spread = jnp.where(sub // 2 == round_index, row, spread)
    local = spread - base
    owned = (local >= 0) & (local < point_count)
    first = jnp.min(jnp.where(owned, lane, 128), axis=1, keepdims=True)
    last = jnp.max(jnp.where(owned, lane, -1), axis=1, keepdims=True)
    second = jnp.where(last > first, last, -1)
    place = jnp.where(sub[:, :1] % 2 == 0, jnp.where(first < 128, first, -1), second)
    here = jnp.sum(jnp.where(lane == place, local, 0), axis=1, keepdims=True)
    columns = iota((8, point_count), 1)
    match = columns == here
    row = jnp.where(lane == 4 * sub + 3, place.astype(f32), 0.0)
    for c in range(points_ref.shape[0]):
        value = jnp.sum(jnp.where(match, points_ref[c : c + 1, :], 0.0), axis=1, keepdims=True)
        row = jnp.where(lane == 4 * sub + c, value, row)
    row = jnp.sum(row, axis=0, keepdims=True)
    out_ref[...] = jnp.broadcast_to(row, out_ref.shape)


def split3(x):
    a = x.astype(bf16).astype(f32)
    rest = x - a
    b = rest.astype(bf16).astype(f32)
    return a, b, rest - b


def eliminate(groups):
    sub, lane = iota((8, 128), 0), iota((8, 128), 1)
    groups = list(groups)
    count = len(groups)
    for b in range(count):
        column = [across_lanes(groups[b], 8 * b + k) for k in range(8)]
        follows = b < count - 1
        inside = (lane >= 8 * b) & (lane < 8 * b + 8)
        rows = jnp.where(inside, jnp.where(lane - 8 * b == sub, 1.0, 0.0).astype(f32), groups[b])
        if follows:
            lower = [across_lanes(groups[b + 1], 8 * b + k) for k in range(8)]
            after = jnp.where(inside, 0.0, groups[b + 1])
        for k in range(8):
            scale = lax.rsqrt(across_rows(column[k], k))
            below = jnp.where(sub > k, column[k] * scale, 0.0)
            pivot_row = across_rows(rows, k) * scale
            factor = {}
            for m in range(k + 1, 8):
                factor[m] = across_rows(column[m], k) * scale
                column[m] = column[m] - below * factor[m]
            rows = jnp.where(sub == k, pivot_row, rows - below * pivot_row)
            if follows:
                multiplier = lower[k] * scale
                for m in range(k + 1, 8):
                    lower[m] = lower[m] - multiplier * factor[m]
                after = after - multiplier * pivot_row
        groups[b] = rows
        if follows:
            groups[b + 1] = after
        if b < count - 2:
            r1, r2, r3 = split3(rows)
            left = jnp.concatenate([r1, r1, r2, r2, r1, r3], 0).astype(bf16)
            right = jnp.concatenate([r1, r2, r1, r2, r3, r1], 0).astype(bf16)
            update = lax.dot_general(
                left, right, (((0,), (0,)), ((), ())), preferred_element_type=f32
            )
            for g in range(b + 2, count):
                groups[g] = jnp.where(inside, 0.0, groups[g]) - update[8 * g : 8 * g + 8, :]
    return groups


def main_kernel(gathered_ref, points_ref, scales_ref, out_ref, matrix, high, low, tall):
    dims, point_count = points_ref.shape
    pivot_count = 128
    rounds = out_ref.shape[0] // pivot_count
    total = rounds * pivot_count
    weights = [root_factor / jnp.full((1, 128), scales_ref[c], f32) for c in range(dims)]
    flipped = jnp.transpose(gathered_ref[...])
    anchor_rows, anchor_columns = [], []
    for r in range(rounds):
        wide = jnp.zeros((4, pivot_count), f32)
        for s in (2 * r, 2 * r + 1):
            fields = flipped[4 * s : 4 * s + 4, :]
            hot = jnp.where(
                fields[3:4, :] == iota((pivot_count, fields.shape[1]), 0).astype(f32), 1.0, 0.0
            ).astype(f32)
            wide = wide + lax.dot_general(
                fields, hot, (((1,), (1,)), ((), ())), precision=HIGHEST, preferred_element_type=f32
            )
        scaled = jnp.concatenate(
            [wide[c : c + 1, :] * weights[c] for c in range(dims)] + [jnp.zeros((5, 128), f32)], 0
        )
        anchor_rows.append(scaled)
        stood = jnp.transpose(jnp.concatenate([scaled] + [jnp.zeros((120, 128), f32)], 0))
        anchor_columns.append(stood[:, :8])
        tall[128 * r : 128 * r + 128, :] = stood[:, :8]

    for r in range(rounds):
        for t in range(r, rounds):
            squared = jnp.zeros((128, 128), f32)
            for c in range(dims):
                offset = anchor_columns[r][:, c : c + 1] - anchor_rows[t][c : c + 1, :]
                squared = squared + offset * offset
            block = jnp.exp2(-squared)
            if t == r:
                diagonal = iota((128, 128), 0) == iota((128, 128), 1)
                block = jnp.where(diagonal, block + nugget_level, block)
            matrix[128 * r : 128 * r + 128, 128 * t : 128 * t + 128] = block
        for t in range(r):
            matrix[128 * r : 128 * r + 128, 128 * t : 128 * t + 128] = jnp.zeros((128, 128), f32)

    keep = iota((128, 128), 0) >= iota((128, 128), 1)
    for r in range(rounds):
        lo, hi = 128 * r, 128 * r + 128
        groups = eliminate([matrix[lo + 8 * g : lo + 8 * g + 8, lo:hi] for g in range(16)])
        inverse = jnp.where(keep, jnp.concatenate(groups, 0), 0.0)
        solved = jnp.dot(inverse, matrix[lo:hi, :], precision=HIGHEST, preferred_element_type=f32)
        matrix[lo:hi, :] = solved
        matrix[lo:hi, lo:hi] = inverse
        for t in range(r + 1, rounds):
            lt, ht = 128 * t, 128 * t + 128
            matrix[lt:ht, lo:hi] = jnp.zeros((128, 128), f32)
            matrix[lt:ht, :] = matrix[lt:ht, :] - lax.dot_general(
                matrix[lo:hi, lt:ht],
                matrix[lo:hi, :],
                (((0,), (0,)), ((), ())),
                precision=HIGHEST,
                preferred_element_type=f32,
            )
    for r in range(rounds):
        lo, hi = 128 * r, 128 * r + 128
        part = matrix[lo:hi, :hi]
        top = part.astype(bf16)
        high[lo:hi, :hi] = top
        low[lo:hi, :hi] = (part - top.astype(f32)).astype(bf16)

    step = 256

    def chunk(i, _):
        at = pl.multiple_of(i * step, step)
        here = [points_ref[c : c + 1, pl.ds(at, step)] * weights[c][:, :1] for c in range(dims)]
        tops, rests = [], []
        for r in range(rounds):
            lo, hi = 128 * r, 128 * r + 128
            squared = jnp.zeros((128, step), f32)
            for c in range(dims):
                offset = tall[lo:hi, c : c + 1] - here[c]
                squared = squared + offset * offset
            value = jnp.exp2(-squared)
            top = value.astype(bf16)
            tops.append(top)
            rests.append((value - top.astype(f32)).astype(bf16))
            k_top = jnp.concatenate(tops, 0)
            k_rest = jnp.concatenate(rests, 0)
            h, l = high[lo:hi, :hi], low[lo:hi, :hi]
            out_ref[lo:hi, pl.ds(at, step)] = (
                jnp.dot(h, k_top, preferred_element_type=f32)
                + jnp.dot(h, k_rest, preferred_element_type=f32)
                + jnp.dot(l, k_top, preferred_element_type=f32)
            )
        return 0

    lax.fori_loop(0, point_count // step, chunk, 0)


def per_device(points, scales, pivots):
    devices = lax.axis_size(("pts", "rep"))
    dims, point_count = points.shape
    rounds, pivot_count = pivots.shape
    place = lax.axis_index(("pts", "rep")).astype(jnp.int32).reshape(1)
    vmem, smem = pl.BlockSpec(memory_space=pltpu.VMEM), pl.BlockSpec(memory_space=pltpu.SMEM)
    packed = pl.pallas_call(
        pack_kernel,
        out_shape=jax.ShapeDtypeStruct((devices, 128), f32),
        in_specs=[smem, vmem, vmem],
        out_specs=vmem,
    )(place, points, pivots)
    gathered = lax.all_to_all(packed, ("pts", "rep"), 0, 0, tiled=True)
    total = rounds * pivot_count
    return pl.pallas_call(
        main_kernel,
        out_shape=jax.ShapeDtypeStruct((total, point_count), f32),
        in_specs=[vmem, vmem, smem],
        out_specs=vmem,
        scratch_shapes=[
            pltpu.VMEM((total, total), f32),
            pltpu.VMEM((total, total), bf16),
            pltpu.VMEM((total, total), bf16),
            pltpu.VMEM((total, 8), f32),
        ],
    )(gathered, points, scales)


def solution(mesh):
    placed = (P(None, ("pts", "rep")), P(), P())
    return jax.shard_map(
        per_device, mesh=mesh, in_specs=placed, out_specs=P(None, ("pts", "rep")), check_vma=False
    )
```

time: 446 us -> 58.7 us (0.13); the launches traced: 438 us -> 58.5 us
  blocking collectives: 276 us -> 29.2 us
  other arithmetic: 108 us -> 0 us
  Pallas kernels: 0 us -> 29.3 us
  local copies, waits for them, and re-layouts: 27.9 us -> 0 us
  matrix products: 25.2 us -> 0 us
    all_gather x4 -> x0, blocking collectives: 276 us -> none  [fetch_rows(): gathered = lax.all_gather(packed, ('pts', 'rep'), axis=1, tiled=True)]
    another operation x20 -> x0, other arithmetic: 92.2 us -> none  [the longest x12 50.4 us: per_device(): factor = jnp.linalg.cholesky(residual)]
    pallas_call x0 -> x2, Pallas kernels: none -> 29.3 us  [the longest x1 27.6 us: per_device(): pl.pallas_call(main_kernel, out_shape=jax.ShapeDtypeStruct((total, point_...]
    all_to_all x0 -> x1, blocking collectives: none -> 29.2 us  [per_device(): gathered = lax.all_to_all(packed, ('pts', 'rep'), 0, 0, tiled=True)]
    dot_general x6 -> x0, matrix products: 18.6 us -> none  [the longest x3 11.9 us: per_device(): jnp.dot(pivot_history.T, previous, precision=lax.Precision.HIGHEST)]
    gather x11 -> x0, local copies, waits for them, and re-layouts: 11.7 us -> none  [the longest x7 7.39 us: select_rows(): source[:, index_list]]
    unnamed x12 -> x0, local copies, waits for them, and re-layouts: 6.69 us -> none
    another operation x4 -> x0, matrix products: 6.58 us -> none  [per_device(): lax.linalg.triangular_solve(factor, columns, left_side=True, lower=True)]
where the time goes in v1:
time: 58.7 us; the launch traced here: 58.5 us
  Pallas kernels  29.3 us (50%)
  blocking collectives  29.2 us (50%)
    all_to_all x1, blocking collectives, per_device(): gathered = lax.all_to_all(packed, ('pts', 'rep'), 0, 0, tiled=True)  29.2 us
    pallas_call x1, Pallas kernels, per_device(): pl.pallas_call(main_kernel, out_shape=jax.ShapeDtypeStruct((total, point_...  27.6 us
    pallas_call x1, Pallas kernels, per_device(): pl.pallas_call(pack_kernel, out_shape=jax.ShapeDtypeStruct((devices, 128)...  1.77 us

profile of v1, /device:TPU:1, one launch (start us, length us, event | category | flops | bytes accessed | tf_op | source)
XLA Modules:
  0.0 58.5 jit_solution(17739428224765759967)
XLA Ops:
  0.0 1.8 %shard_map.37 = f32[256,128]{1,0:T(8,128)} custom-call(s32[1]{0:T(128)} %bitcast.place_ref, f32[3,2048]{1,0:T(4,128)} %points_ref.3, s32[4,128]{1,0:T(4,128)} %pivots_ref.1), custom_call_target="tpu_custom_call" | custom-call | tf_op jit(solution)/shard_map/pallas_call | solution.py:203
  1.8 29.2 %all_to_all.11 = f32[256,1,128]{2,1,0:T(1,128)} all-to-all(f32[256,1,128]{2,1,0:T(1,128)} %bitcast.6), channel_id=1, replica_groups=mesh['pts'=128,'rep'=2] {'pts','rep'}, dimensions={0} | all-to-all | bytes 262144 | tf_op jit(solution)/shard_map/all_to_all | solution.py:209
  30.9 27.6 %shard_map.38 = f32[512,2048]{1,0:T(8,128)} custom-call(f32[256,128]{1,0:T(8,128)} %bitcast.5, f32[3,2048]{1,0:T(4,128)} %points_ref.3, f32[3]{0:T(128)} %scales_ref.1), custom_call_target="tpu_custom_call" | custom-call | tf_op jit(solution)/shard_map/pallas_call | solution.py:211

commit v2 on v1

v2 whole, which is shorter than its diff:
```python
import functools
import math

import jax
import jax.numpy as jnp
from jax import lax
from jax.experimental import pallas as pl
from jax.experimental.pallas import tpu as pltpu
from jax.sharding import PartitionSpec as P

nugget_level = 0.1
root_factor = math.sqrt(0.5 * math.log2(math.e))
f32 = jnp.float32
bf16 = jnp.bfloat16
HIGHEST = lax.Precision.HIGHEST


def iota(shape, axis):
    return lax.broadcasted_iota(jnp.int32, shape, axis)


def across_lanes(x, j):
    return jnp.broadcast_to(x[:, j : j + 1], (8, 128))


def across_rows(x, k):
    return jnp.broadcast_to(x[k : k + 1, :], (8, 128))


def pack_kernel(place_ref, points_ref, pivots_ref, out_ref):
    point_count = points_ref.shape[1]
    base = place_ref[0] * point_count
    sub, lane = iota((8, 128), 0), iota((8, 128), 1)
    spread = jnp.zeros((8, 128), jnp.int32)
    for round_index in range(pivots_ref.shape[0]):
        row = jnp.broadcast_to(pivots_ref[round_index : round_index + 1, :], (8, 128))
        spread = jnp.where(sub // 2 == round_index, row, spread)
    local = spread - base
    owned = (local >= 0) & (local < point_count)
    first = jnp.min(jnp.where(owned, lane, 128), axis=1, keepdims=True)
    last = jnp.max(jnp.where(owned, lane, -1), axis=1, keepdims=True)
    second = jnp.where(last > first, last, -1)
    place = jnp.where(sub[:, :1] % 2 == 0, jnp.where(first < 128, first, -1), second)
    here = jnp.sum(jnp.where(lane == place, local, 0), axis=1, keepdims=True)
    columns = iota((8, point_count), 1)
    match = columns == here
    row = jnp.where(lane == 4 * sub + 3, place.astype(f32), 0.0)
    for c in range(points_ref.shape[0]):
        value = jnp.sum(jnp.where(match, points_ref[c : c + 1, :], 0.0), axis=1, keepdims=True)
        row = jnp.where(lane == 4 * sub + c, value, row)
    row = jnp.sum(row, axis=0, keepdims=True)
    out_ref[...] = jnp.broadcast_to(row, out_ref.shape)


def split3(x):
    a = x.astype(bf16).astype(f32)
    rest = x - a
    b = rest.astype(bf16).astype(f32)
    return a, b, rest - b


def eliminate(groups):
    sub, lane = iota((8, 128), 0), iota((8, 128), 1)
    count = len(groups)
    for b in range(count):
        column = [across_lanes(groups[b], 8 * b + k) for k in range(8)]
        follows = b < count - 1
        inside = (lane >= 8 * b) & (lane < 8 * b + 8)
        rows = jnp.where(inside, jnp.where(lane - 8 * b == sub, 1.0, 0.0).astype(f32), groups[b])
        final = rows
        if follows:
            lower = [across_lanes(groups[b + 1], 8 * b + k) for k in range(8)]
            after = jnp.where(inside, 0.0, groups[b + 1])
        for k in range(0, 8, 2):
            a = across_rows(column[k], k)
            side = across_rows(column[k], k + 1)
            c = across_rows(column[k + 1], k + 1)
            root = lax.rsqrt(a * c - side * side)
            scale = root * root
            masked0 = jnp.where(sub > k + 1, column[k], 0.0)
            masked1 = jnp.where(sub > k + 1, column[k + 1], 0.0)
            raw0 = masked0 * c - masked1 * side
            raw1 = masked1 * a - masked0 * side
            below0, below1 = raw0 * scale, raw1 * scale
            picks = {}
            for m in range(k + 2, 8):
                picks[m] = (across_rows(column[k], m), across_rows(column[k + 1], m))
                p0, p1 = picks[m]
                if m < k + 4:
                    column[m] = column[m] - (raw0 * p0 + raw1 * p1) * scale
                else:
                    column[m] = column[m] - (below0 * p0 + below1 * p1)
            row0, row1 = across_rows(rows, k), across_rows(rows, k + 1)
            if follows:
                next0 = (lower[k] * c - lower[k + 1] * side) * scale
                next1 = (lower[k + 1] * a - lower[k] * side) * scale
                for m in range(k + 2, 8):
                    p0, p1 = picks[m]
                    lower[m] = lower[m] - (next0 * p0 + next1 * p1)
                after = after - (next0 * row0 + next1 * row1)
            if k < 6:
                rows = rows - (below0 * row0 + below1 * row1)
            first = lax.rsqrt(a)
            ratio = side * (first * first)
            final = jnp.where(sub == k, row0 * first, final)
            final = jnp.where(sub == k + 1, (row1 - row0 * ratio) * (root * (a * first)), final)
            if follows and k == 6:
                groups[b + 1] = after
            yield
        groups[b] = final
        if b < count - 2:
            r1, r2, r3 = split3(final)
            left = jnp.concatenate([r1, r1, r2, r2, r1, r3], 0).astype(bf16)
            right = jnp.concatenate([r1, r2, r1, r2, r3, r1], 0).astype(bf16)
            update = lax.dot_general(
                left, right, (((0,), (0,)), ((), ())), preferred_element_type=f32
            )
            for g in range(b + 2, count):
                groups[g] = jnp.where(inside, 0.0, groups[g]) - update[8 * g : 8 * g + 8, :]


def split2(x):
    top = x.astype(bf16)
    return top, (x - top.astype(f32)).astype(bf16)


def squares(columns, rows):
    total = None
    for c in range(3):
        offset = columns[:, c : c + 1] - rows[c]
        total = offset * offset if total is None else total + offset * offset
    return total


def outer(left, right):
    return lax.dot_general(
        left, right, (((0,), (0,)), ((), ())), precision=HIGHEST, preferred_element_type=f32
    )


def main_kernel(
    gathered_ref, points_ref, scales_ref, out_ref, matrix, near, tall, solved, stack, ready, lows, done
):
    dims, point_count = points_ref.shape
    rounds = out_ref.shape[0] // 128
    step = 256
    chunks = point_count // step
    weights = [root_factor / jnp.full((1, 128), scales_ref[c], f32) for c in range(dims)]
    flipped = jnp.transpose(gathered_ref[...])
    anchors = []
    for r in range(rounds):
        wide = jnp.zeros((16, 128), f32)
        for s in (2 * r, 2 * r + 1):
            fields = flipped[4 * s : 4 * s + 4, :]
            places = iota((128, fields.shape[1]), 0).astype(f32)
            hot = jnp.where(fields[3:4, :] == places, 1.0, 0.0).astype(bf16)
            parts = split3(fields)
            parts = jnp.concatenate(list(parts) + [parts[0]], 0).astype(bf16)
            wide = wide + lax.dot_general(
                parts, hot, (((1,), (1,)), ((), ())), preferred_element_type=f32
            )
        wide = (wide[0:4, :] + wide[4:8, :]) + wide[8:12, :]
        scaled = jnp.concatenate(
            [wide[c : c + 1, :] * weights[c] for c in range(dims)] + [jnp.zeros((5, 128), f32)], 0
        )
        anchors.append([scaled[c : c + 1, :] for c in range(dims)])
        tall[128 * r : 128 * r + 128, :] = jnp.transpose(
            jnp.concatenate([scaled] + [jnp.zeros((120, 128), f32)], 0)
        )[:, :8]
    for c in range(dims):
        near[c : c + 1, :] = points_ref[c : c + 1, :] * weights[c][:, :1]

    def fill(r, t):
        block = jnp.exp2(-squares(tall[128 * r : 128 * r + 128, :], anchors[t]))
        if t == r:
            diagonal = iota((128, 128), 0) == iota((128, 128), 1)
            block = jnp.where(diagonal, block + nugget_level, block)
        matrix[128 * r : 128 * r + 128, 128 * t : 128 * t + 128] = block

    def block(r, t):
        return matrix[128 * r : 128 * r + 128, 128 * t : 128 * t + 128]

    def columns_task(r, j, part):
        span = slice(j * step, j * step + step)
        size = 128 // 4
        lo = size * part
        value = jnp.exp2(
            -squares(
                tall[128 * r + lo : 128 * r + lo + size, :],
                [near[c : c + 1, span] for c in range(dims)],
            )
        )
        if r > 0:
            value = value - jnp.dot(
                lows[lo : lo + size, 384 * OFFSET[r] : 384 * (OFFSET[r] + r)],
                stack[: 384 * r, span],
                preferred_element_type=f32,
            )
        top, rest = split2(value)
        ready[lo : lo + size, span] = top
        ready[128 + lo : 128 + lo + size, span] = rest
        ready[256 + lo : 256 + lo + size, span] = top

    def solve_task(r, j, inverses):
        span = slice(j * step, j * step + step)
        value = jnp.dot(inverses, ready[:, span], preferred_element_type=f32)
        solved[128 * r : 128 * r + 128, span] = value
        if r < rounds - 1:
            top, rest = split2(value)
            stack[384 * r : 384 * r + 128, span] = top
            stack[384 * r + 128 : 384 * r + 256, span] = rest
            stack[384 * r + 256 : 384 * r + 384, span] = top

    def copy_out(r):
        return pltpu.make_async_copy(
            solved.at[pl.ds(128 * r, 128), :], out_ref.at[pl.ds(128 * r, 128), :], done.at[r]
        )

    def flip_task(s, t):
        top, rest = split2(jnp.transpose(block(s, t)))
        at = 384 * (OFFSET[t] + s)
        lows[:, at : at + 128] = top
        lows[:, at + 128 : at + 256] = top
        lows[:, at + 256 : at + 384] = rest

    def subtract_task(s, t, u):
        matrix[128 * t : 128 * t + 128, 128 * u : 128 * u + 128] = block(t, u) - outer(
            block(s, t), block(s, u)
        )

    keep = iota((128, 128), 0) >= iota((128, 128), 1)
    fill(0, 0)
    inverse = inverses = None
    for r in range(rounds):
        tasks = []
        if r == 0:
            tasks += [functools.partial(fill, t, u) for t in range(rounds) for u in range(t, rounds) if u]
        else:
            s = r - 1
            for u in range(r + 1, rounds):
                tasks.append(functools.partial(widen, s, u, inverse))
            tasks += [functools.partial(flip_task, s, t) for t in range(r, rounds)]
            tasks += [
                functools.partial(subtract_task, s, t, u)
                for t in range(r, rounds)
                for u in range(t, rounds)
                if u > r
            ]
        for j in range(chunks):
            if r > 0:
                tasks.append(functools.partial(solve_task, r - 1, j, inverses))
            for part in range(4):
                tasks.append(functools.partial(columns_task, r, j, part))
        groups = [matrix[128 * r + 8 * g : 128 * r + 8 * g + 8, 128 * r : 128 * r + 128] for g in range(16)]
        at, slots = 0, 64
        for slot, _ in enumerate(eliminate(groups)):
            until = (slot + 1) * len(tasks) // slots
            while at < until:
                tasks[at]()
                at += 1
        inverse = jnp.where(keep, jnp.concatenate(groups, 0), 0.0)
        top, rest = split2(inverse)
        inverses = jnp.concatenate([top, top, rest], 1)

        def widen(s, u, inverse):
            matrix[128 * s : 128 * s + 128, 128 * u : 128 * u + 128] = jnp.dot(
                inverse, block(s, u), precision=HIGHEST, preferred_element_type=f32
            )

        if r > 0:
            copy_out(r - 1).start()
        if r < rounds - 1:
            widen(r, r + 1, inverse)
            subtract_task(r, r + 1, r + 1)
    for j in range(chunks):
        solve_task(rounds - 1, j, inverses)
    copy_out(rounds - 1).start()
    for r in range(rounds):
        copy_out(r).wait()


OFFSET = [0, 0, 1, 3]


def per_device(points, scales, pivots):
    devices = lax.axis_size(("pts", "rep"))
    dims, point_count = points.shape
    rounds, pivot_count = pivots.shape
    place = lax.axis_index(("pts", "rep")).astype(jnp.int32).reshape(1)
    vmem, smem = pl.BlockSpec(memory_space=pltpu.VMEM), pl.BlockSpec(memory_space=pltpu.SMEM)
    packed = pl.pallas_call(
        pack_kernel,
        out_shape=jax.ShapeDtypeStruct((devices, 128), f32),
        in_specs=[smem, vmem, vmem],
        out_specs=vmem,
    )(place, points, pivots)
    gathered = lax.all_to_all(packed, ("pts", "rep"), 0, 0, tiled=True)
    total = rounds * pivot_count
    return pl.pallas_call(
        main_kernel,
        out_shape=jax.ShapeDtypeStruct((total, point_count), f32),
        in_specs=[vmem, vmem, smem],
        out_specs=pl.BlockSpec(memory_space=pl.ANY),
        scratch_shapes=[
            pltpu.VMEM((total, total), f32),
            pltpu.VMEM((8, point_count), f32),
            pltpu.VMEM((total, 8), f32),
            pltpu.VMEM((total, point_count), f32),
            pltpu.VMEM((384 * (rounds - 1), point_count), bf16),
            pltpu.VMEM((384, point_count), bf16),
            pltpu.VMEM((128, 384 * 6), bf16),
            pltpu.SemaphoreType.DMA((rounds,)),
        ],
    )(gathered, points, scales)


def solution(mesh):
    placed = (P(None, ("pts", "rep")), P(), P())
    return jax.shard_map(
        per_device, mesh=mesh, in_specs=placed, out_specs=P(None, ("pts", "rep")), check_vma=False
    )
```

time: 58.7 us -> 53.2 us (0.906)
  Pallas kernels: 29.3 us -> 23.6 us
    pallas_call x1, Pallas kernels: 27.6 us -> 21.9 us  [per_device(): pl.pallas_call(main_kernel, out_shape=jax.ShapeDtypeStruct((total, point_...]
where the time goes in v2:
time: 53.2 us; the launch traced here: 53 us
  blocking collectives  29.2 us (55%)
  Pallas kernels  23.6 us (44%)
    all_to_all x1, blocking collectives, per_device(): gathered = lax.all_to_all(packed, ('pts', 'rep'), 0, 0, tiled=True)  29.2 us
    pallas_call x1, Pallas kernels, per_device(): pl.pallas_call(main_kernel, out_shape=jax.ShapeDtypeStruct((total, point_...  21.9 us
    pallas_call x1, Pallas kernels, per_device(): pl.pallas_call(pack_kernel, out_shape=jax.ShapeDtypeStruct((devices, 128)...  1.77 us

profile of v2, /device:TPU:1, one launch (start us, length us, event | category | flops | bytes accessed | tf_op | source)
XLA Modules:
  0.0 53.0 jit_solution(6948196288629520740)
XLA Ops:
  0.0 1.8 %shard_map.37 = f32[256,128]{1,0:T(8,128)} custom-call(s32[1]{0:T(128)} %bitcast.place_ref, f32[3,2048]{1,0:T(4,128)} %points_ref.3, s32[4,128]{1,0:T(4,128)} %pivots_ref.1), custom_call_target="tpu_custom_call" | custom-call | tf_op jit(solution)/shard_map/pallas_call | solution.py:291
  1.8 29.2 %all_to_all.11 = f32[256,1,128]{2,1,0:T(1,128)} all-to-all(f32[256,1,128]{2,1,0:T(1,128)} %bitcast.6), channel_id=1, replica_groups=mesh['pts'=128,'rep'=2] {'pts','rep'}, dimensions={0} | all-to-all | bytes 262144 | tf_op jit(solution)/shard_map/all_to_all | solution.py:297
  30.9 21.9 %shard_map.38 = f32[512,2048]{1,0:T(8,128)} custom-call(f32[256,128]{1,0:T(8,128)} %bitcast.5, f32[3,2048]{1,0:T(4,128)} %points_ref.3, f32[3]{0:T(128)} %scales_ref.1), custom_call_target="tpu_custom_call" | custom-call | tf_op jit(solution)/shard_map/pallas_call | solution.py:299

commit v3 on v2

--- a/solution.py
+++ b/solution.py
@@ -59,37 +59,45 @@
     return a, b, rest - b
 
 
+def total_of(terms):
+    while len(terms) > 1:
+        terms = [a + b for a, b in zip(terms[::2], terms[1::2])]
+    return terms[0]
 def eliminate(groups):
     sub, lane = iota((8, 128), 0), iota((8, 128), 1)
+    odd = sub % 2 == 1
+    pair = sub // 2
     count = len(groups)
     for b in range(count):
         column = [across_lanes(groups[b], 8 * b + k) for k in range(8)]
         follows = b < count - 1
         inside = (lane >= 8 * b) & (lane < 8 * b + 8)
         rows = jnp.where(inside, jnp.where(lane - 8 * b == sub, 1.0, 0.0).astype(f32), groups[b])
-        final = rows
         if follows:
             lower = [across_lanes(groups[b + 1], 8 * b + k) for k in range(8)]
             after = jnp.where(inside, 0.0, groups[b + 1])
+        final = rows
+        coefs = []
         for k in range(0, 8, 2):
+            mine = pair == k // 2
             a = across_rows(column[k], k)
             side = across_rows(column[k], k + 1)
             c = across_rows(column[k + 1], k + 1)
             root = lax.rsqrt(a * c - side * side)
             scale = root * root
-            masked0 = jnp.where(sub > k + 1, column[k], 0.0)
-            masked1 = jnp.where(sub > k + 1, column[k + 1], 0.0)
+            masked0 = jnp.where(mine, 0.0, column[k])
+            masked1 = jnp.where(mine, 0.0, column[k + 1])
             raw0 = masked0 * c - masked1 * side
             raw1 = masked1 * a - masked0 * side
-            below0, below1 = raw0 * scale, raw1 * scale
-            picks = {}
+            part0, part1 = raw0 * scale, raw1 * scale
+            coefs.append((a * scale, side * scale, c * scale))
+            picks = {m: (across_rows(column[k], m), across_rows(column[k + 1], m)) for m in range(k + 2, 8)}
             for m in range(k + 2, 8):
-                picks[m] = (across_rows(column[k], m), across_rows(column[k + 1], m))
                 p0, p1 = picks[m]
                 if m < k + 4:
                     column[m] = column[m] - (raw0 * p0 + raw1 * p1) * scale
                 else:
-                    column[m] = column[m] - (below0 * p0 + below1 * p1)
+                    column[m] = column[m] - (part0 * p0 + part1 * p1)
             row0, row1 = across_rows(rows, k), across_rows(rows, k + 1)
             if follows:
                 next0 = (lower[k] * c - lower[k + 1] * side) * scale
@@ -98,25 +106,27 @@
                     p0, p1 = picks[m]
                     lower[m] = lower[m] - (next0 * p0 + next1 * p1)
                 after = after - (next0 * row0 + next1 * row1)
-            if k < 6:
-                rows = rows - (below0 * row0 + below1 * row1)
+            rows = rows - (part0 * row0 + part1 * row1)
             first = lax.rsqrt(a)
             ratio = side * (first * first)
             final = jnp.where(sub == k, row0 * first, final)
             final = jnp.where(sub == k + 1, (row1 - row0 * ratio) * (root * (a * first)), final)
-            if follows and k == 6:
-                groups[b + 1] = after
-            yield
+            if k == 6:
+                if follows: groups[b + 1] = after
+            else: yield
         groups[b] = final
-        if b < count - 2:
-            r1, r2, r3 = split3(final)
-            left = jnp.concatenate([r1, r1, r2, r2, r1, r3], 0).astype(bf16)
-            right = jnp.concatenate([r1, r2, r1, r2, r3, r1], 0).astype(bf16)
-            update = lax.dot_general(
-                left, right, (((0,), (0,)), ((), ())), preferred_element_type=f32
-            )
-            for g in range(b + 2, count):
-                groups[g] = jnp.where(inside, 0.0, groups[g]) - update[8 * g : 8 * g + 8, :]
+        start = b + 2
+        if start < count:
+            spread = []
+            for k in range(0, 8, 2):
+                row0, row1 = across_rows(rows, k), across_rows(rows, k + 1)
+                lead, side, tail = coefs[k // 2]
+                spread += [row0 * tail - row1 * side, row1 * lead - row0 * side]
+            far = list(range(b + 2, count))
+            whole = [[across_lanes(groups[g], 8 * b + k) for g in far] for k in range(8)]
+            for i, g in enumerate(far):
+                groups[g] = jnp.where(inside, 0.0, groups[g]) - total_of([whole[k][i] * spread[k] for k in range(8)])
+        yield
 
 
 def split2(x):
@@ -139,7 +149,7 @@
 
 
 def main_kernel(
-    gathered_ref, points_ref, scales_ref, out_ref, matrix, near, tall, solved, stack, ready, lows, done
+    gathered_ref, points_ref, scales_ref, out_ref, matrix, near, tall, signs, solved, stack, ready, lows, done
 ):
     dims, point_count = points_ref.shape
     rounds = out_ref.shape[0] // 128
@@ -147,6 +157,7 @@
     chunks = point_count // step
     weights = [root_factor / jnp.full((1, 128), scales_ref[c], f32) for c in range(dims)]
     flipped = jnp.transpose(gathered_ref[...])
+    sub8 = iota((8, 128), 0)
     anchors = []
     for r in range(rounds):
         wide = jnp.zeros((16, 128), f32)
@@ -160,15 +171,26 @@
                 parts, hot, (((1,), (1,)), ((), ())), preferred_element_type=f32
             )
         wide = (wide[0:4, :] + wide[4:8, :]) + wide[8:12, :]
-        scaled = jnp.concatenate(
-            [wide[c : c + 1, :] * weights[c] for c in range(dims)] + [jnp.zeros((5, 128), f32)], 0
+        scaled = [(wide[c : c + 1, :] - 0.5) * weights[c] for c in range(dims)]
+        anchors.append(scaled)
+        norm = -(scaled[0] * scaled[0] + scaled[1] * scaled[1] + scaled[2] * scaled[2])
+        block8 = jnp.where(sub8 == 3, 1.0, jnp.where(sub8 == 4, norm, 0.0))
+        for c in range(dims):
+            block8 = jnp.where(sub8 == c, scaled[c], block8)
+        q1, q2, q3 = split3(block8)
+        stood = jnp.transpose(
+            jnp.concatenate([q1, q1, q2, q2, q1, q3, q2, q3, block8, jnp.zeros((56, 128), f32)], 0)
         )
-        anchors.append([scaled[c : c + 1, :] for c in range(dims)])
-        tall[128 * r : 128 * r + 128, :] = jnp.transpose(
-            jnp.concatenate([scaled] + [jnp.zeros((120, 128), f32)], 0)
-        )[:, :8]
+        tall[128 * r : 128 * r + 128, :] = stood[:, 64:72]
+        signs[128 * r : 128 * r + 128, :] = stood[:, :64].astype(bf16)
+    wide8 = (8, point_count)
+    here = [(points_ref[c : c + 1, :] - 0.5) * weights[c][:, :1] for c in range(dims)]
+    norm = -(here[0] * here[0] + here[1] * here[1] + here[2] * here[2])
+    block8 = jnp.where(iota(wide8, 0) == 4, 1.0, jnp.where(iota(wide8, 0) == 3, norm, 0.0))
     for c in range(dims):
-        near[c : c + 1, :] = points_ref[c : c + 1, :] * weights[c][:, :1]
+        block8 = jnp.where(iota(wide8, 0) == c, here[c] + here[c], block8)
+    p1, p2, p3 = split3(block8)
+    near[...] = jnp.concatenate([p1, p2, p1, p2, p3, p1, p3, p2], 0).astype(bf16)
 
     def fill(r, t):
         block = jnp.exp2(-squares(tall[128 * r : 128 * r + 128, :], anchors[t]))
@@ -180,26 +202,23 @@
     def block(r, t):
         return matrix[128 * r : 128 * r + 128, 128 * t : 128 * t + 128]
 
-    def columns_task(r, j, part):
+    def columns_task(r, j):
         span = slice(j * step, j * step + step)
-        size = 128 // 4
-        lo = size * part
         value = jnp.exp2(
-            -squares(
-                tall[128 * r + lo : 128 * r + lo + size, :],
-                [near[c : c + 1, span] for c in range(dims)],
+            jnp.dot(
+                signs[128 * r : 128 * r + 128, :], near[:, span], preferred_element_type=f32
             )
         )
         if r > 0:
             value = value - jnp.dot(
-                lows[lo : lo + size, 384 * OFFSET[r] : 384 * (OFFSET[r] + r)],
+                lows[:, 384 * OFFSET[r] : 384 * (OFFSET[r] + r)],
                 stack[: 384 * r, span],
                 preferred_element_type=f32,
             )
         top, rest = split2(value)
-        ready[lo : lo + size, span] = top
-        ready[128 + lo : 128 + lo + size, span] = rest
-        ready[256 + lo : 256 + lo + size, span] = top
+        ready[:128, span] = top
+        ready[128:256, span] = rest
+        ready[256:, span] = top
 
     def solve_task(r, j, inverses):
         span = slice(j * step, j * step + step)
@@ -249,8 +268,7 @@
         for j in range(chunks):
             if r > 0:
                 tasks.append(functools.partial(solve_task, r - 1, j, inverses))
-            for part in range(4):
-                tasks.append(functools.partial(columns_task, r, j, part))
+            tasks.append(functools.partial(columns_task, r, j))
         groups = [matrix[128 * r + 8 * g : 128 * r + 8 * g + 8, 128 * r : 128 * r + 128] for g in range(16)]
         at, slots = 0, 64
         for slot, _ in enumerate(eliminate(groups)):
@@ -303,8 +321,9 @@
         out_specs=pl.BlockSpec(memory_space=pl.ANY),
         scratch_shapes=[
             pltpu.VMEM((total, total), f32),
-            pltpu.VMEM((8, point_count), f32),
+            pltpu.VMEM((64, point_count), bf16),
             pltpu.VMEM((total, 8), f32),
+            pltpu.VMEM((total, 64), bf16),
             pltpu.VMEM((total, point_count), f32),
             pltpu.VMEM((384 * (rounds - 1), point_count), bf16),
             pltpu.VMEM((384, point_count), bf16),

time: 53.2 us -> 49.5 us (0.930)
  Pallas kernels: 23.6 us -> 20.1 us
    pallas_call x1, Pallas kernels: 21.9 us -> 18.4 us  [per_device(): pl.pallas_call(main_kernel, out_shape=jax.ShapeDtypeStruct((total, point_...]
where the time goes in v3:
time: 49.5 us; the launch traced here: 49.3 us
  blocking collectives  29.2 us (59%)
  Pallas kernels  20.1 us (41%)
    all_to_all x1, blocking collectives, per_device(): gathered = lax.all_to_all(packed, ('pts', 'rep'), 0, 0, tiled=True)  29.2 us
    pallas_call x1, Pallas kernels, per_device(): pl.pallas_call(main_kernel, out_shape=jax.ShapeDtypeStruct((total, point_...  18.4 us
    pallas_call x1, Pallas kernels, per_device(): pl.pallas_call(pack_kernel, out_shape=jax.ShapeDtypeStruct((devices, 128)...  1.77 us

profile of v3, /device:TPU:1, one launch (start us, length us, event | category | flops | bytes accessed | tf_op | source)
XLA Modules:
  0.0 49.3 jit_solution(659847381542805783)
XLA Ops:
  0.0 1.8 %shard_map.37 = f32[256,128]{1,0:T(8,128)} custom-call(s32[1]{0:T(128)} %bitcast.place_ref, f32[3,2048]{1,0:T(4,128)} %points_ref.3, s32[4,128]{1,0:T(4,128)} %pivots_ref.1), custom_call_target="tpu_custom_call" | custom-call | tf_op jit(solution)/shard_map/pallas_call | solution.py:309
  1.8 29.2 %all_to_all.11 = f32[256,1,128]{2,1,0:T(1,128)} all-to-all(f32[256,1,128]{2,1,0:T(1,128)} %bitcast.6), channel_id=1, replica_groups=mesh['pts'=128,'rep'=2] {'pts','rep'}, dimensions={0} | all-to-all | bytes 262144 | tf_op jit(solution)/shard_map/all_to_all | solution.py:315
  30.9 18.4 %shard_map.38 = f32[512,2048]{1,0:T(8,128)} custom-call(f32[256,128]{1,0:T(8,128)} %bitcast.5, f32[3,2048]{1,0:T(4,128)} %points_ref.3, f32[3]{0:T(128)} %scales_ref.1), custom_call_target="tpu_custom_call" | custom-call | tf_op jit(solution)/shard_map/pallas_call | solution.py:317

commit v4 on v3

--- a/solution.py
+++ b/solution.py
@@ -63,13 +63,19 @@
     while len(terms) > 1:
         terms = [a + b for a, b in zip(terms[::2], terms[1::2])]
     return terms[0]
+def total_of(terms):
+    while len(terms) > 1:
+        terms = [a + b for a, b in zip(terms[::2], terms[1::2])]
+    return terms[0]
 def eliminate(groups):
     sub, lane = iota((8, 128), 0), iota((8, 128), 1)
     odd = sub % 2 == 1
     pair = sub // 2
     count = len(groups)
+    zero = groups[0] * 0.0
     for b in range(count):
         column = [across_lanes(groups[b], 8 * b + k) for k in range(8)]
+        column[0], column[1] = column[0] + zero, column[1] + zero
         follows = b < count - 1
         inside = (lane >= 8 * b) & (lane < 8 * b + 8)
         rows = jnp.where(inside, jnp.where(lane - 8 * b == sub, 1.0, 0.0).astype(f32), groups[b])
@@ -142,14 +148,28 @@
     return total
 
 
+def left_terms(x, axis):
+    a, b, c = split3(x)
+    return jnp.concatenate([a, a, b, b, a, c], axis).astype(bf16)
+
+
+def right_terms(y):
+    a, b, c = split3(y)
+    return jnp.concatenate([a, b, a, b, c, a], 0).astype(bf16)
+
+
 def outer(left, right):
     return lax.dot_general(
-        left, right, (((0,), (0,)), ((), ())), precision=HIGHEST, preferred_element_type=f32
+        left_terms(left, 0),
+        right_terms(right),
+        (((0,), (0,)), ((), ())),
+        preferred_element_type=f32,
     )
 
 
 def main_kernel(
-    gathered_ref, points_ref, scales_ref, out_ref, matrix, near, tall, signs, solved, stack, ready, lows, done
+    gathered_ref, points_ref, scales_ref, out_ref, matrix, near, tall, signs, solved, stack, ready, lows,
+    inverses, panel, done, last
 ):
     dims, point_count = points_ref.shape
     rounds = out_ref.shape[0] // 128
@@ -157,9 +177,18 @@
     chunks = point_count // step
     weights = [root_factor / jnp.full((1, 128), scales_ref[c], f32) for c in range(dims)]
     flipped = jnp.transpose(gathered_ref[...])
-    sub8 = iota((8, 128), 0)
-    anchors = []
-    for r in range(rounds):
+    anchors = {}
+
+    def coordinates(scaled, place, scale):
+        wide = (8, scaled[0].shape[1])
+        sub = iota(wide, 0)
+        norm = -(scaled[0] * scaled[0] + scaled[1] * scaled[1] + scaled[2] * scaled[2])
+        block8 = jnp.where(sub == 7 - place, 1.0, jnp.where(sub == place, norm, 0.0))
+        for c in range(dims):
+            block8 = jnp.where(sub == c, scaled[c] * scale, block8)
+        return block8
+
+    def anchor_task(r):
         wide = jnp.zeros((16, 128), f32)
         for s in (2 * r, 2 * r + 1):
             fields = flipped[4 * s : 4 * s + 4, :]
@@ -172,25 +201,20 @@
             )
         wide = (wide[0:4, :] + wide[4:8, :]) + wide[8:12, :]
         scaled = [(wide[c : c + 1, :] - 0.5) * weights[c] for c in range(dims)]
-        anchors.append(scaled)
-        norm = -(scaled[0] * scaled[0] + scaled[1] * scaled[1] + scaled[2] * scaled[2])
-        block8 = jnp.where(sub8 == 3, 1.0, jnp.where(sub8 == 4, norm, 0.0))
-        for c in range(dims):
-            block8 = jnp.where(sub8 == c, scaled[c], block8)
+        anchors[r] = scaled
+        block8 = coordinates(scaled, 4, 1.0)
         q1, q2, q3 = split3(block8)
         stood = jnp.transpose(
             jnp.concatenate([q1, q1, q2, q2, q1, q3, q2, q3, block8, jnp.zeros((56, 128), f32)], 0)
         )
         tall[128 * r : 128 * r + 128, :] = stood[:, 64:72]
         signs[128 * r : 128 * r + 128, :] = stood[:, :64].astype(bf16)
-    wide8 = (8, point_count)
-    here = [(points_ref[c : c + 1, :] - 0.5) * weights[c][:, :1] for c in range(dims)]
-    norm = -(here[0] * here[0] + here[1] * here[1] + here[2] * here[2])
-    block8 = jnp.where(iota(wide8, 0) == 4, 1.0, jnp.where(iota(wide8, 0) == 3, norm, 0.0))
-    for c in range(dims):
-        block8 = jnp.where(iota(wide8, 0) == c, here[c] + here[c], block8)
-    p1, p2, p3 = split3(block8)
-    near[...] = jnp.concatenate([p1, p2, p1, p2, p3, p1, p3, p2], 0).astype(bf16)
+
+    def near_task(j):
+        span = slice(j * 2 * step, (j + 1) * 2 * step)
+        here = [(points_ref[c : c + 1, span] - 0.5) * weights[c][:, :1] for c in range(dims)]
+        p1, p2, p3 = split3(coordinates(here, 3, 2.0))
+        near[:, span] = jnp.concatenate([p1, p2, p1, p2, p3, p1, p3, p2], 0).astype(bf16)
 
     def fill(r, t):
         block = jnp.exp2(-squares(tall[128 * r : 128 * r + 128, :], anchors[t]))
@@ -220,9 +244,13 @@
         ready[128:256, span] = rest
         ready[256:, span] = top
 
-    def solve_task(r, j, inverses):
+    def solve_task(r, j):
         span = slice(j * step, j * step + step)
-        value = jnp.dot(inverses, ready[:, span], preferred_element_type=f32)
+        value = jnp.dot(
+            inverses[128 * (r % 2) : 128 * (r % 2) + 128, :],
+            ready[:, span],
+            preferred_element_type=f32,
+        )
         solved[128 * r : 128 * r + 128, span] = value
         if r < rounds - 1:
             top, rest = split2(value)
@@ -235,6 +263,10 @@
             solved.at[pl.ds(128 * r, 128), :], out_ref.at[pl.ds(128 * r, 128), :], done.at[r]
         )
 
+    def copy_last(j):
+        rows, columns = pl.ds(128 * (rounds - 1), 128), pl.ds(j * step, step)
+        return pltpu.make_async_copy(solved.at[rows, columns], out_ref.at[rows, columns], last.at[j])
+
     def flip_task(s, t):
         top, rest = split2(jnp.transpose(block(s, t)))
         at = 384 * (OFFSET[t] + s)
@@ -247,56 +279,86 @@
             block(s, t), block(s, u)
         )
 
+    def widen_task(s, u, inverse):
+        matrix[128 * s : 128 * s + 128, 128 * u : 128 * u + 128] = jnp.dot(
+            left_terms(inverse, 1), right_terms(block(s, u)), preferred_element_type=f32
+        )
+
+    def panel_task(r):
+        panel[...] = right_terms(block(r, r + 1))
+
+    def quarter_task(r, q, rows):
+        lo = 32 * q
+        at = 128 * (r % 2) + lo
+        top, rest = split2(rows)
+        inverses[at : at + 32, :] = jnp.concatenate([top, top, rest], 1)
+        if r < rounds - 1:
+            wide = jnp.dot(left_terms(rows, 1), panel[...], preferred_element_type=f32)
+            matrix[128 * r + lo : 128 * r + lo + 32, 128 * (r + 1) : 128 * (r + 2)] = wide
+            after = slice(128 * (r + 1), 128 * (r + 2))
+            matrix[after, after] = matrix[after, after] - outer(wide, wide)
+
     keep = iota((128, 128), 0) >= iota((128, 128), 1)
+    anchor_task(0)
     fill(0, 0)
-    inverse = inverses = None
+    inverse = None
+    task = functools.partial
     for r in range(rounds):
-        tasks = []
+        urgent, tasks = [], []
         if r == 0:
-            tasks += [functools.partial(fill, t, u) for t in range(rounds) for u in range(t, rounds) if u]
+            urgent += [task(anchor_task, 1), task(fill, 0, 1), task(panel_task, 0), task(fill, 1, 1)]
+            tasks += [task(near_task, j) for j in range(chunks // 2)]
+            tasks += [task(anchor_task, t) for t in range(2, rounds)]
+            tasks += [task(fill, t, u) for u in range(2, rounds) for t in range(u + 1)]
         else:
             s = r - 1
-            for u in range(r + 1, rounds):
-                tasks.append(functools.partial(widen, s, u, inverse))
-            tasks += [functools.partial(flip_task, s, t) for t in range(r, rounds)]
+            if r < rounds - 1:
+                urgent += [task(widen_task, s, r + 1, inverse), task(subtract_task, s, r, r + 1)]
+                urgent += [task(panel_task, r), task(subtract_task, s, r + 1, r + 1)]
+            urgent.append(task(flip_task, s, r))
+            tasks += [task(widen_task, s, u, inverse) for u in range(r + 2, rounds)]
+            tasks += [task(flip_task, s, t) for t in range(r + 1, rounds)]
             tasks += [
-                functools.partial(subtract_task, s, t, u)
-                for t in range(r, rounds)
-                for u in range(t, rounds)
-                if u > r
+                task(subtract_task, s, t, u) for t in range(r, rounds) for u in range(max(t, r + 2), rounds)
             ]
         for j in range(chunks):
             if r > 0:
-                tasks.append(functools.partial(solve_task, r - 1, j, inverses))
-            tasks.append(functools.partial(columns_task, r, j))
-        groups = [matrix[128 * r + 8 * g : 128 * r + 8 * g + 8, 128 * r : 128 * r + 128] for g in range(16)]
-        at, slots = 0, 64
+                tasks.append(task(solve_task, r - 1, j))
+            tasks.append(task(columns_task, r, j))
+        groups = [
+            matrix[128 * r + 8 * g : 128 * r + 8 * g + 8, 128 * r : 128 * r + 128] for g in range(16)
+        ]
+        finished = []
+        at = 0
         for slot, _ in enumerate(eliminate(groups)):
-            until = (slot + 1) * len(tasks) // slots
-            while at < until:
-                tasks[at]()
-                at += 1
-        inverse = jnp.where(keep, jnp.concatenate(groups, 0), 0.0)
-        top, rest = split2(inverse)
-        inverses = jnp.concatenate([top, top, rest], 1)
-
-        def widen(s, u, inverse):
-            matrix[128 * s : 128 * s + 128, 128 * u : 128 * u + 128] = jnp.dot(
-                inverse, block(s, u), precision=HIGHEST, preferred_element_type=f32
-            )
-
+            if urgent:
+                urgent.pop(0)()
+            else:
+                share = (slot + 1) / 64
+                until = len(tasks) * (SLOPE * share + (1 - SLOPE) * share * share)
+                while at < until - 1e-6:
+                    tasks[at]()
+                    at += 1
+            if slot % 16 == 15:
+                q = slot // 16
+                rows = jnp.where(
+                    keep[32 * q : 32 * q + 32, :], jnp.concatenate(groups[4 * q : 4 * q + 4], 0), 0.0
+                )
+                finished.append(rows)
+                quarter_task(r, q, rows)
+        inverse = jnp.concatenate(finished, 0)
         if r > 0:
             copy_out(r - 1).start()
-        if r < rounds - 1:
-            widen(r, r + 1, inverse)
-            subtract_task(r, r + 1, r + 1)
     for j in range(chunks):
-        solve_task(rounds - 1, j, inverses)
-    copy_out(rounds - 1).start()
-    for r in range(rounds):
+        solve_task(rounds - 1, j)
+        copy_last(j).start()
+    for r in range(rounds - 1):
         copy_out(r).wait()
-
-
+    for j in range(chunks):
+        copy_last(j).wait()
+
+
+SLOPE = 0.5
 OFFSET = [0, 0, 1, 3]
 
 
@@ -328,7 +390,10 @@
             pltpu.VMEM((384 * (rounds - 1), point_count), bf16),
             pltpu.VMEM((384, point_count), bf16),
             pltpu.VMEM((128, 384 * 6), bf16),
-            pltpu.SemaphoreType.DMA((rounds,)),
+            pltpu.VMEM((256, 384), bf16),
+            pltpu.VMEM((768, 128), bf16),
+            pltpu.SemaphoreType.DMA((rounds - 1,)),
+            pltpu.SemaphoreType.DMA((point_count // 256,)),
         ],
     )(gathered, points, scales)
 

time: 49.5 us -> 46.9 us (0.947)
  Pallas kernels: 20.1 us -> 17.6 us
    pallas_call x1, Pallas kernels: 18.4 us -> 15.8 us  [per_device(): pl.pallas_call(main_kernel, out_shape=jax.ShapeDtypeStruct((total, point_...]
where the time goes in v4:
time: 46.9 us; the launch traced here: 46.8 us
  blocking collectives  29.2 us (62%)
  Pallas kernels  17.6 us (38%)
    all_to_all x1, blocking collectives, per_device(): gathered = lax.all_to_all(packed, ('pts', 'rep'), 0, 0, tiled=True)  29.2 us
    pallas_call x1, Pallas kernels, per_device(): pl.pallas_call(main_kernel, out_shape=jax.ShapeDtypeStruct((total, point_...  15.8 us
    pallas_call x1, Pallas kernels, per_device(): pl.pallas_call(pack_kernel, out_shape=jax.ShapeDtypeStruct((devices, 128)...  1.77 us

profile of v4, /device:TPU:1, one launch (start us, length us, event | category | flops | bytes accessed | tf_op | source)
XLA Modules:
  0.0 46.8 jit_solution(9914135014268329236)
XLA Ops:
  0.0 1.8 %shard_map.37 = f32[256,128]{1,0:T(8,128)} custom-call(s32[1]{0:T(128)} %bitcast.place_ref, f32[3,2048]{1,0:T(4,128)} %points_ref.3, s32[4,128]{1,0:T(4,128)} %pivots_ref.1), custom_call_target="tpu_custom_call" | custom-call | tf_op jit(solution)/shard_map/pallas_call | solution.py:371
  1.8 29.2 %all_to_all.11 = f32[256,1,128]{2,1,0:T(1,128)} all-to-all(f32[256,1,128]{2,1,0:T(1,128)} %bitcast.6), channel_id=1, replica_groups=mesh['pts'=128,'rep'=2] {'pts','rep'}, dimensions={0} | all-to-all | bytes 262144 | tf_op jit(solution)/shard_map/all_to_all | solution.py:377
  30.9 15.8 %shard_map.38 = f32[512,2048]{1,0:T(8,128)} custom-call(f32[256,128]{1,0:T(8,128)} %bitcast.5, f32[3,2048]{1,0:T(4,128)} %points_ref.3, f32[3]{0:T(128)} %scales_ref.1), custom_call_target="tpu_custom_call" | custom-call | tf_op jit(solution)/shard_map/pallas_call | solution.py:379

commit v5 on v4

--- a/solution.py
+++ b/solution.py
@@ -173,7 +173,7 @@
 ):
     dims, point_count = points_ref.shape
     rounds = out_ref.shape[0] // 128
-    step = 256
+    step = 512
     chunks = point_count // step
     weights = [root_factor / jnp.full((1, 128), scales_ref[c], f32) for c in range(dims)]
     flipped = jnp.transpose(gathered_ref[...])
@@ -211,7 +211,7 @@
         signs[128 * r : 128 * r + 128, :] = stood[:, :64].astype(bf16)
 
     def near_task(j):
-        span = slice(j * 2 * step, (j + 1) * 2 * step)
+        span = slice(j * step, (j + 1) * step)
         here = [(points_ref[c : c + 1, span] - 0.5) * weights[c][:, :1] for c in range(dims)]
         p1, p2, p3 = split3(coordinates(here, 3, 2.0))
         near[:, span] = jnp.concatenate([p1, p2, p1, p2, p3, p1, p3, p2], 0).astype(bf16)
@@ -307,7 +307,7 @@
         urgent, tasks = [], []
         if r == 0:
             urgent += [task(anchor_task, 1), task(fill, 0, 1), task(panel_task, 0), task(fill, 1, 1)]
-            tasks += [task(near_task, j) for j in range(chunks // 2)]
+            tasks += [task(near_task, j) for j in range(chunks)]
             tasks += [task(anchor_task, t) for t in range(2, rounds)]
             tasks += [task(fill, t, u) for u in range(2, rounds) for t in range(u + 1)]
         else:
@@ -393,7 +393,7 @@
             pltpu.VMEM((256, 384), bf16),
             pltpu.VMEM((768, 128), bf16),
             pltpu.SemaphoreType.DMA((rounds - 1,)),
-            pltpu.SemaphoreType.DMA((point_count // 256,)),
+            pltpu.SemaphoreType.DMA((point_count // 512,)),
         ],
     )(gathered, points, scales)
 

time: 46.9 us -> 47 us (level)
  no operation moved by 1% of the time
where the time goes in v5:
time: 47 us; the launch traced here: 46.9 us
  blocking collectives  29.2 us (62%)
  Pallas kernels  17.7 us (38%)
    all_to_all x1, blocking collectives, per_device(): gathered = lax.all_to_all(packed, ('pts', 'rep'), 0, 0, tiled=True)  29.2 us
    pallas_call x1, Pallas kernels, per_device(): pl.pallas_call(main_kernel, out_shape=jax.ShapeDtypeStruct((total, point_...  15.9 us
    pallas_call x1, Pallas kernels, per_device(): pl.pallas_call(pack_kernel, out_shape=jax.ShapeDtypeStruct((devices, 128)...  1.77 us

profile of v5, /device:TPU:1, one launch (start us, length us, event | category | flops | bytes accessed | tf_op | source)
XLA Modules:
  0.0 46.9 jit_solution(10757751916233008950)
XLA Ops:
  0.0 1.8 %shard_map.37 = f32[256,128]{1,0:T(8,128)} custom-call(s32[1]{0:T(128)} %bitcast.place_ref, f32[3,2048]{1,0:T(4,128)} %points_ref.3, s32[4,128]{1,0:T(4,128)} %pivots_ref.1), custom_call_target="tpu_custom_call" | custom-call | tf_op jit(solution)/shard_map/pallas_call | solution.py:371
  1.8 29.2 %all_to_all.11 = f32[256,1,128]{2,1,0:T(1,128)} all-to-all(f32[256,1,128]{2,1,0:T(1,128)} %bitcast.6), channel_id=1, replica_groups=mesh['pts'=128,'rep'=2] {'pts','rep'}, dimensions={0} | all-to-all | bytes 262144 | tf_op jit(solution)/shard_map/all_to_all | solution.py:377
  30.9 15.9 %shard_map.38 = f32[512,2048]{1,0:T(8,128)} custom-call(f32[256,128]{1,0:T(8,128)} %bitcast.5, f32[3,2048]{1,0:T(4,128)} %points_ref.3, f32[3]{0:T(128)} %scales_ref.1), custom_call_target="tpu_custom_call" | custom-call | tf_op jit(solution)/shard_map/pallas_call | solution.py:379
